TPU v7x, 32 devices: a whole 2x2x4 slice. The times are simulated.
32 devices in a mesh: sec: 2 (over y), dev: 16 (over z, x, core).
Axes of the slice: x: 2, y: 2, z: 4, core: 2. Of those that a mesh axis runs over, the one named last changes fastest.
Arguments:
- flow_state: float32 [5, 8, 1024, 512], P(None, None, ('sec', 'dev')), may hold values from -6 to 6
- diffusion: float32 [8, 1024, 512], P(None, ('sec', 'dev')), may hold values from 0.02 to 0.1
- wall_stress: float32 [2, 1024, 512], P(None, ('sec', 'dev')), may hold values from -3 to 3
- batch_counts: int32 [32, 48], P(('sec', 'dev')), may hold values from 1 to 4, 120 in all within a row
- batch_routes: int32 [1536, 1], P(('sec', 'dev')), may hold values from 0 to 31; in each aligned block of 48 rows (0 to 47, 48 to 95, ...) at most 2 rows name the same one
- wall_index: int32 [1536, 4], P(('sec', 'dev')), may hold values from 0 to 16383, as said below
- input_weight: bfloat16 [12, 2048], replicated, may hold values from -1.75 to 1.75
- middle_weight: bfloat16 [2048, 2048], P(('sec', 'dev')), may hold values from -0.125 to 0.125
- output_weight: bfloat16 [2, 2048], replicated, may hold values from -0.125 to 0.125
Outputs:
- new_field: float32 [5, 8, 1024, 512], P(None, None, ('sec', 'dev'))
- new_stress: float32 [2, 1024, 512], P(None, ('sec', 'dev'))
- batch_loss: float32 [32], P(('sec', 'dev'))
- grad_w_in: float32 [12, 2048], replicated
- grad_w_mid: float32 [2048, 2048], P(('sec', 'dev'))
Inputs may be any that keep to these rules, and one draw needn't show every extreme that they name: `batch_routes`: within the 48 rows of one device no trainer is named more than 2 times, and every trainer is named by some row. `batch_counts`: each device's row sums to 120. `wall_index`: all entries of the 48 rows of one device are distinct.
All inputs are finite; a program needn't handle non-finite values.
Results may differ from a plain program's by a relative error of at most 0.00091.
Values may be sent and summed in bfloat16 or wider, within the bound.
No kernel may reach another device: no remote copies, remote signals or barrier semaphores. Data moves between devices by JAX's collectives and lax.ppermute only.
A program may use at most 128 MiB of HBM per device.

v0:
```python
import math
import jax
import jax.numpy as jnp
from jax import lax
from jax.sharding import PartitionSpec as P

SLOTS = 2
advect_number = 0.3
wall_gain = 0.5
grad_number = 32.0


def extended(block, sides, width):
    for axis, dim in sides:
        count = lax.axis_size(axis)
        forward = [(i, i + 1) for i in range(count - 1)]
        forward.append((count - 1, 0))
        backward = [(target, source) for source, target in forward]
        low = lax.ppermute(
            lax.slice_in_dim(block, block.shape[dim] - width, None, axis=dim), axis, forward
        )
        high = lax.ppermute(lax.slice_in_dim(block, 0, width, axis=dim), axis, backward)
        block = jnp.concatenate([low, block, high], axis=dim)
    return block


def advance(flow_state, diffusion, below_z, above_z):
    below_x = jnp.concatenate([flow_state[..., :1], flow_state[..., :-1]], axis=3)
    above_x = jnp.concatenate([flow_state[..., 1:], flow_state[..., -1:]], axis=3)
    below_y = jnp.concatenate([flow_state[:, :1], flow_state[:, :-1]], axis=1)
    above_y = jnp.concatenate([flow_state[:, 1:], flow_state[:, -1:]], axis=1)
    spread = below_x + above_x + below_y + above_y + below_z + above_z - 6.0 * flow_state
    return flow_state + advect_number * (below_x - flow_state) + diffusion[None] * spread


def wall_columns(flow_state):
    points = flow_state.shape[2] * flow_state.shape[3]
    inputs = flow_state[0:4, 0:3].reshape(12, points)
    targets = jnp.stack(
        [flow_state[1, 4] - flow_state[1, 3], flow_state[3, 4] - flow_state[3, 3]]
    ).reshape(2, points)
    return jnp.concatenate([inputs, targets], axis=0).astype(jnp.bfloat16)


def apply_wall(advanced, new_stress):
    advanced = advanced.at[1, 0].add(-wall_gain * new_stress[0])
    return advanced.at[3, 0].add(-wall_gain * new_stress[1])


def contract_first(left, right):
    return lax.dot_general(
        left, right, (((0,), (0,)), ((), ())), preferred_element_type=jnp.float32
    )


def contract_last(left, right):
    return lax.dot_general(
        left, right, (((1,), (1,)), ((), ())), preferred_element_type=jnp.float32
    )


def body(
    flow_state,
    diffusion,
    wall_stress,
    batch_counts,
    batch_routes,
    wall_index,
    input_weight,
    middle_weight,
    output_weight,
):
    tile_count, capacity = wall_index.shape
    devices = lax.axis_size(("sec", "dev"))
    channels = 14
    slot_total = devices * SLOTS
    row_total = slot_total * capacity
    points = flow_state.shape[2] * flow_state.shape[3]
    columns = wall_columns(flow_state)
    picked = jnp.take(columns, wall_index.reshape(-1), axis=1).reshape(
        channels, tile_count, capacity
    )
    is_live = (
        jnp.arange(capacity, dtype=jnp.int32)[None, :] < batch_counts.reshape(tile_count)[:, None]
    )
    picked = jnp.where(is_live[None], picked, jnp.zeros((), jnp.bfloat16))
    destination = batch_routes.reshape(tile_count)
    matches = (destination[:, None] == jnp.arange(devices, dtype=jnp.int32)[None, :]).astype(
        jnp.int32
    )
    slot_rank = jnp.sum((jnp.cumsum(matches, axis=0) - matches) * matches, axis=1)
    slot_id = destination * SLOTS + slot_rank
    placing = (slot_id[:, None] == jnp.arange(slot_total, dtype=jnp.int32)[None, :]).astype(
        jnp.bfloat16
    )
    send_rows = jnp.einsum(
        "bs,cbk->sck", placing, picked, preferred_element_type=jnp.float32
    ).astype(jnp.bfloat16)
    send_rows = send_rows.reshape(devices, SLOTS, channels, capacity)
    send_live = jnp.einsum(
        "bs,bk->sk", placing, is_live.astype(jnp.bfloat16), preferred_element_type=jnp.float32
    ).astype(jnp.bfloat16)
    send_live = send_live.reshape(devices, SLOTS, capacity)
    got_rows, got_live = (
        lax.all_to_all(send_rows, ("sec", "dev"), split_axis=0, concat_axis=0, tiled=True),
        lax.all_to_all(send_live, ("sec", "dev"), split_axis=0, concat_axis=0, tiled=True),
    )
    sample_rows = jnp.transpose(got_rows, (0, 1, 3, 2)).reshape(row_total, channels)
    features = sample_rows[:, :12]
    targets = sample_rows[:, 12:].astype(jnp.float32)
    live_rows = got_live.reshape(row_total).astype(jnp.float32)
    pre_first = jnp.dot(features, input_weight, preferred_element_type=jnp.float32)
    first_tanh = jnp.tanh(pre_first)
    first_act = first_tanh.astype(jnp.bfloat16)
    part = first_act
    pre_second = jnp.dot(
        part,
        lax.all_gather(middle_weight, ("sec", "dev"), axis=0, tiled=True),
        preferred_element_type=jnp.float32,
    )
    second_tanh = jnp.tanh(pre_second)
    second_act = second_tanh.astype(jnp.bfloat16)
    prediction = contract_last(second_act, output_weight)
    errors = (prediction - targets) * live_rows[:, None]
    sent_back = jnp.transpose(
        prediction.astype(jnp.bfloat16).reshape(devices, SLOTS, capacity, 2), (0, 1, 3, 2)
    )
    answers = lax.all_to_all(sent_back, ("sec", "dev"), split_axis=0, concat_axis=0, tiled=True)
    answers = answers.reshape(slot_total, 2, capacity)
    live_total = jnp.sum(live_rows)
    batch_loss = (0.5 * jnp.sum(errors * errors) / live_total).reshape(1)
    live_dev = 5 * tile_count * capacity // 8
    scale = grad_number / math.sqrt(live_dev * devices)
    back_out = (errors * scale).astype(jnp.bfloat16)
    back_second = (
        jnp.dot(back_out, output_weight, preferred_element_type=jnp.float32)
        * (1.0 - second_tanh * second_tanh)
    ).astype(jnp.bfloat16)
    back_hidden = contract_last(
        back_second, lax.all_gather(middle_weight, ("sec", "dev"), axis=0, tiled=True)
    )
    back_first = (back_hidden * (1.0 - first_tanh * first_tanh)).astype(jnp.bfloat16)
    part = first_act
    grad_w_mid = lax.psum_scatter(
        contract_first(part, back_second), ("sec", "dev"), scatter_dimension=0, tiled=True
    )
    grad_w_in = lax.psum(contract_first(features, back_first), ("sec", "dev"))
    per_tile = jnp.einsum("bs,sck->cbk", placing, answers, preferred_element_type=jnp.float32)
    target_index = jnp.where(is_live, wall_index, points).reshape(-1)
    new_stress = (
        wall_stress.reshape(2, points)
        .at[:, target_index]
        .set(per_tile.reshape(2, -1), mode="drop")
        .reshape(wall_stress.shape)
    )
    padded = extended(flow_state.astype(jnp.bfloat16), ((("sec", "dev"), 2),), 1).astype(
        flow_state.dtype
    )
    advanced = advance(flow_state, diffusion, padded[:, :, :-2], padded[:, :, 2:])
    new_field = apply_wall(advanced, new_stress)
    return (new_field, new_stress, batch_loss, grad_w_in, grad_w_mid)


def solution(mesh):
    in_specs = (
        P(None, None, ("sec", "dev"), None),
        P(None, ("sec", "dev"), None),
        P(None, ("sec", "dev"), None),
        P(("sec", "dev"), None),
        P(("sec", "dev"), None),
        P(("sec", "dev"), None),
        P(),
        P(("sec", "dev"), None),
        P(),
    )
    out_specs = (
        P(None, None, ("sec", "dev"), None),
        P(None, ("sec", "dev"), None),
        P(("sec", "dev")),
        P(),
        P(("sec", "dev"), None),
    )
    return jax.shard_map(body, mesh=mesh, in_specs=in_specs, out_specs=out_specs, check_vma=False)
```

profile of v0, /device:TPU:9, one launch (start us, length us, event | category | flops | bytes accessed | tf_op | source)
XLA Modules:
  0.0 425.7 jit_solution(3434637611886213195)
XLA Ops:
  11.9 6.3 %all-to-all-start.2 = ((bf16[32,2,4]{2,1,0:T(2,128)(2,1)}), bf16[32,2,4]{2,1,0:T(2,128)(2,1)S(1)}, u32[]{:S(2)}, u32[]{:S(2)}) async-start(bf16[32,2,4]{2,1,0:T(2,128)(2,1)} %bitcast.18), calls=%async_computation.2 | async-start | bytes 32768 | tf_op jit(solution)/shard_map/all_to_all | solution.py:106
  19.1 2.0 convert_element_type.52
  22.9 3.4 copy.38
  26.3 3.4 gather_fusion
  30.8 5.8 %all-to-all-start = ((bf16[32,2,14,4]{2,1,3,0:T(2,128)(2,1)}), bf16[32,2,14,4]{2,1,3,0:T(2,128)(2,1)S(1)}, u32[]{:S(2)}, u32[]{:S(2)}) async-start(bf16[32,2,14,4]{2,1,3,0:T(2,128)(2,1)} %copy.41), calls=%async_computation | async-start | bytes 131072 | tf_op jit(solution)/shard_map/all_to_all | solution.py:105
  36.9 5.8 %all-to-all-done = bf16[32,2,14,4]{2,1,3,0:T(2,128)(2,1)S(1)} async-done(((bf16[32,2,14,4]{2,1,3,0:T(2,128)(2,1)}), bf16[32,2,14,4]{2,1,3,0:T(2,128)(2,1)S(1)}, u32[]{:S(2)}, u32[]{:S(2)}) %all-to-all-start) | async-done | bytes 7200 | tf_op jit(solution)/shard_map/all_to_all | solution.py:105
  42.9 1.8 convolution_tanh_fusion.1
  44.6 44.9 %all-gather.2.cloned.1.call-done = bf16[2048,2048]{1,0:T(8,128)(2,1)} async-done(((bf16[64,2048]{1,0:T(8,128)(2,1)}), bf16[2048,2048]{1,0:T(8,128)(2,1)}) %all-gather.2.cloned.1.call-update) | async-done | bytes 8388624 | tf_op jit(solution)/shard_map/all_gather | solution.py:118
  89.6 6.4 %convolution_tanh_fusion = f32[256,2048]{1,0:T(8,128)S(1)} fusion(bf16[2048,2048]{1,0:T(8,128)(2,1)} %all-gather.2.cloned.1.call-done, f32[256,2048]{1,0:T(8,128)} %convolution_tanh_fusion.1), kind=kOutput, calls=%fused_computation.8 | convolution fusion | flops 2148007936 | bytes 12582912 | tf_op jit(solution)/shard_map/dot_general | solution.py:116
  98.4 7.4 %fusion.9 = f32[12,2048]{1,0:T(8,128)} fusion(bf16[256,2048]{1,0:T(8,128)(2,1)} %fusion.8, bf16[2048,2048]{1,0:T(8,128)(2,1)} %all-gather.2.cloned.1.call-done, f32[256,2048]{1,0:T(8,128)} %convolution_tanh_fusion.1, bf16[256,14]{1,0:T(8,128)(2,1)S(1)} %bitcast.59), kind=kOutput, calls=%fused_computation.22 | convolution fusion | flops 2162163712 | bytes 11639808 | tf_op jit(solution)/shard_map/dot_general | solution.py:51
  105.9 10.0 %fusion.13 = f32[2048,2048]{1,0:T(8,128)} fusion(bf16[256,2048]{1,0:T(8,128)(2,1)} %fusion.8, f32[256,2048]{1,0:T(8,128)} %convolution_tanh_fusion.1), kind=kOutput, calls=%fused_computation.30 | convolution fusion | flops 2148007936 | bytes 19922944 | tf_op jit(solution)/shard_map/dot_general | solution.py:51
  118.7 4.6 %copy.35 = f32[2,32,512]{0,2,1:T(8,128)} copy(f32[2,32,512]{2,1,0:T(8,128)S(1)} %copy-done.5) | data formatting | bytes 262144 | tf_op args[2]
  125.4 2.8 fusion.43
  128.2 3.4 fusion.42
  132.3 3.4 maximum_convert_fusion
  136.4 6.6 %all-to-all-start.1 = ((bf16[32,2,2,4]{3,1,2,0:T(2,128)(2,1)}), bf16[32,2,2,4]{3,1,2,0:T(2,128)(2,1)S(1)}, u32[]{:S(2)}, u32[]{:S(2)}) async-start(bf16[32,2,2,4]{3,1,2,0:T(2,128)(2,1)} %copy.43), calls=%async_computation.1 | async-start | bytes 65536 | tf_op jit(solution)/shard_map/all_to_all | solution.py:128
  143.1 9.2 %fusion.4 = f32[5,8,32,512]{3,2,1,0:T(8,128)} fusion(f32[5,8,34,512]{3,2,1,0:T(8,128)} %maximum_convert_fusion, f32[5,8,32,1]{3,2,1,0:T(8,128)} %get-tuple-element.49, f32[5,8,32,511]{3,2,1,0:T(8,128)} %get-tuple-element.51, f32[5,7,32,512]{3,2,1,0:T(8,128)} %get-tuple-element.53, f32[5,1,32,512]{3,2,1,0:T(8,128)} %get-tuple-element.55, ...), kind=kLoop, calls=%fused_computation.13 | loop fusion | flops 10485760 | bytes 21495808 | tf_op jit(solution)/shard_map/add | solution.py:33
  154.2 7.6 %scatter_fusion = f32[2,16384]{0,1:T(8,128)} fusion(f32[2,16384]{0,1:T(8,128)} %bitcast.52, s32[192]{0:T(256)S(1)} %bitcast.68, f32[192,2]{1,0:T(8,128)S(1)} %copy.47), kind=kCustom, calls=%fused_computation.1 | custom fusion | bytes 5376 | tf_op jit(solution)/shard_map/scatter | solution.py:153
  161.8 5.9 %copy.50 = f32[2,32,512]{2,1,0:T(8,128)} copy(f32[2,32,512]{0,2,1:T(8,128)} %bitcast.53) | data formatting | bytes 262144
  167.7 12.3 %fusion = (f32[16384]{0:T(1024)S(1)}, f32[16384]{0:T(1024)S(1)}) fusion(f32[2,16384]{0,1:T(8,128)} %scatter_fusion), kind=kLoop, calls=%fused_computation.3 | loop fusion | flops 32768 | bytes 262144 | tf_op jit(solution)/shard_map/mul | solution.py:47
  180.0 1.5 fusion.17
  183.0 43.7 %all-reduce.2.cloned.1.call-done = f32[12,2048]{1,0:T(8,128)} async-done(((f32[12,2048]{1,0:T(8,128)}), f32[12,2048]{1,0:T(8,128)}) %all-reduce.2.cloned.1.call-update) | async-done | bytes 98320 | tf_op jit(solution)/shard_map/psum | solution.py:147
  226.7 189.8 %reduce-scatter.2.cloned.1.call-done = f32[64,2048]{1,0:T(8,128)} async-done(((f32[2048,2048]{1,0:T(8,128)}), f32[64,2048]{1,0:T(8,128)}) %reduce-scatter.2.cloned.1.call-update) | async-done | bytes 524304 | tf_op jit(solution)/shard_map/reduce_scatter | solution.py:144
  416.5 1.6 copy.60
  (76 shorter events, 19.6 us)
Async XLA Ops:
  7.2 35.7 %copy-start = (bf16[12,2048]{1,0:T(8,128)(2,1)S(1)}, bf16[12,2048]{1,0:T(8,128)(2,1)}, u32[]{:S(2)}) copy-start(bf16[12,2048]{1,0:T(8,128)(2,1)} %param.19) | copy-start | bytes 147460
  7.2 13.9 %copy-start.2 = (f32[5,8,32,512]{3,2,1,0:T(8,128)S(1)}, f32[5,8,32,512]{3,2,1,0:T(8,128)}, u32[]{:S(2)}) copy-start(f32[5,8,32,512]{3,2,1,0:T(8,128)} %param.13) | copy-start | bytes 7864324
  7.2 82.4 %all-gather.2.cloned.1.call-start = ((), (), s32[]{:S(2)}) async-start(), calls=%async_computation.4 | async-start | bytes 8650752 | tf_op jit(solution)/shard_map/all_gather | solution.py:118
  11.9 19.0 %all-to-all-start.2 = ((bf16[32,2,4]{2,1,0:T(2,128)(2,1)}), bf16[32,2,4]{2,1,0:T(2,128)(2,1)S(1)}, u32[]{:S(2)}, u32[]{:S(2)}) async-start(bf16[32,2,4]{2,1,0:T(2,128)(2,1)} %bitcast.18), calls=%async_computation.2 | async-start | bytes 32768 | tf_op jit(solution)/shard_map/all_to_all | solution.py:106
  21.1 1.2 copy-start.3
  22.9 6.9 %copy-start.7 = (s32[48,4]{0,1:T(4,128)S(1)}, s32[48,4]{0,1:T(4,128)}, u32[]{:S(2)}) copy-start(s32[48,4]{0,1:T(4,128)} %param.18) | copy-start | bytes 2308
  22.9 6.9 %copy-start.8 = (s32[1,48]{1,0:T(1,128)S(1)}, s32[1,48]{1,0:T(1,128)}, u32[]{:S(2)}) copy-start(s32[1,48]{1,0:T(1,128)} %param.16) | copy-start | bytes 580
  30.8 11.8 %all-to-all-start = ((bf16[32,2,14,4]{2,1,3,0:T(2,128)(2,1)}), bf16[32,2,14,4]{2,1,3,0:T(2,128)(2,1)S(1)}, u32[]{:S(2)}, u32[]{:S(2)}) async-start(bf16[32,2,14,4]{2,1,3,0:T(2,128)(2,1)} %copy.41), calls=%async_computation | async-start | bytes 131072 | tf_op jit(solution)/shard_map/all_to_all | solution.py:105
  36.7 190.0 %all-reduce.2.cloned.1.call-start = ((), (), s32[]{:S(2)}) async-start(), calls=%async_computation.5 | async-start | bytes 262144 | tf_op jit(solution)/shard_map/psum | solution.py:147
  44.6 51.3 %copy-start.6 = (bf16[2,2048]{1,0:T(2,128)(2,1)S(1)}, bf16[2,2048]{1,0:T(2,128)(2,1)}, u32[]{:S(2)}) copy-start(bf16[2,2048]{1,0:T(2,128)(2,1)} %param.21) | copy-start | bytes 24580
  105.9 310.7 %reduce-scatter.2.cloned.1.call-start = ((), (), s32[]{:S(2)}) async-start(), calls=%async_computation.6 | async-start | bytes 17301504 | tf_op jit(solution)/shard_map/reduce_scatter | solution.py:144
  115.9 2.8 copy-start.5
  117.2 15.1 %collective-permute-start = (bf16[5,8,1,512]{3,2,1,0:T(2,128)(2,1)S(1)}, bf16[5,8,1,512]{3,2,1,0:T(2,128)(2,1)}, u32[]{:S(2)}, u32[]{:S(2)}) collective-permute-start(bf16[5,8,1,512]{3,2,1,0:T(2,128)(2,1)S(1)} %get-tuple-element.56), channel_id=1, source_target_pairs={{0,1},{1,2},{2,3},{3,4},{4,5},{5,6},{6,7},{7,8},{8,9},{9,10},{10,1... | collective-permute-start | bytes 122888 | tf_op jit(solution)/shard_map/ppermute | solution.py:19
  118.5 13.8 %collective-permute-start.1 = (bf16[5,8,1,512]{3,2,1,0:T(2,128)(2,1)S(1)}, bf16[5,8,1,512]{3,2,1,0:T(2,128)(2,1)}, u32[]{:S(2)}, u32[]{:S(2)}) collective-permute-start(bf16[5,8,1,512]{3,2,1,0:T(2,128)(2,1)S(1)} %get-tuple-element.57), channel_id=1, source_target_pairs={{1,0},{2,1},{3,2},{4,3},{5,4},{6,5},{7,6},{8,7},{9,8},{10,9},{11,1... | collective-permute-start | bytes 122888 | tf_op jit(solution)/shard_map/ppermute | solution.py:22
  128.2 4.1 copy-start.4
  136.4 17.2 %all-to-all-start.1 = ((bf16[32,2,2,4]{3,1,2,0:T(2,128)(2,1)}), bf16[32,2,2,4]{3,1,2,0:T(2,128)(2,1)S(1)}, u32[]{:S(2)}, u32[]{:S(2)}) async-start(bf16[32,2,2,4]{3,1,2,0:T(2,128)(2,1)} %copy.43), calls=%async_computation.1 | async-start | bytes 65536 | tf_op jit(solution)/shard_map/all_to_all | solution.py:128
  167.7 250.4 %copy-start.1 = (bf16[12,2048]{1,0:T(8,128)(2,1)S(1)}, bf16[12,2048]{1,0:T(8,128)(2,1)}, u32[]{:S(2)}) copy-start(bf16[12,2048]{1,0:T(8,128)(2,1)} %param.19) | copy-start | bytes 147460
Sparse Core Ops, SparseCore 0:
  10.8 78.7 all-gather.1
  106.0 120.6 all-reduce.1
  229.6 186.8 reduce-scatter.1
where the time goes:
time: 426 us
  waiting for transfers between devices  285 us (67%)
  local copies, waits for them, and re-layouts  41.6 us (10%)
  other arithmetic  33.1 us (8%)
  matrix products  29.2 us (7%)
  starting transfers between devices  20.3 us (5%)
  between operations  16.5 us (4%)
    reduce_scatter x1, waiting for transfers between devices, body(): lax.psum_scatter(contract_first(part, back_second), ('sec', 'dev'), scatt...  190 us
    all_gather x1, waiting for transfers between devices, body(): lax.all_gather(middle_weight, ('sec', 'dev'), axis=0, tiled=True)  44.9 us
    psum x1, waiting for transfers between devices, body(): grad_w_in = lax.psum(contract_first(features, back_first), ('sec', 'dev'))  43.7 us
    dot_general x2, matrix products, contract_first(): lax.dot_general(left, right, (((0,), (0,)), ((), ())), preferred_element_...  17.4 us
    unnamed x27, local copies, waits for them, and re-layouts  14.4 us
    mul x1, other arithmetic, apply_wall(): return advanced.at[3, 0].add(-wall_gain * new_stress[1])  12.3 us
    add x1, other arithmetic, advance(): flow_state + advect_number * (below_x - flow_state)  9.22 us
  transfers between devices with their start and end apart: 8, of which 4 were waited for; matrix products, arithmetic and copies ran while one was open for 20% of the time, Pallas kernels for 0%

commit v1 on v0

--- a/solution.py
+++ b/solution.py
@@ -144,7 +144,9 @@
     grad_w_mid = lax.psum_scatter(
         contract_first(part, back_second), ("sec", "dev"), scatter_dimension=0, tiled=True
     )
-    grad_w_in = lax.psum(contract_first(features, back_first), ("sec", "dev"))
+    grad_w_in = jnp.sum(
+        lax.all_gather(contract_first(features, back_first), ("sec", "dev")), axis=0
+    )
     per_tile = jnp.einsum("bs,sck->cbk", placing, answers, preferred_element_type=jnp.float32)
     target_index = jnp.where(is_live, wall_index, points).reshape(-1)
     new_stress = (

time: 426 us -> 362 us (0.85)
  waiting for transfers between devices: 285 us -> 218 us
    psum x1 -> x0, waiting for transfers between devices: 43.7 us -> none  [body(): grad_w_in = lax.psum(contract_first(features, back_first), ('sec', 'dev'))]
    reduce_scatter x1, waiting for transfers between devices: 190 us -> 167 us  [body(): lax.psum_scatter(contract_first(part, back_second), ('sec', 'dev'), scatt...]
    unnamed x27 -> x26, local copies, waits for them, and re-layouts: 14.4 us -> 12.9 us
  transfers between devices with their start and end apart: 8 -> 8, of which waited for: 4 -> 3; matrix products, arithmetic and copies ran while one was open for 20% -> 25% of each run, Pallas kernels for 0% -> 0%
where the time goes in v1:
time: 362 us; the launch traced here: 361 us
  waiting for transfers between devices  218 us (60%)
  local copies, waits for them, and re-layouts  40.1 us (11%)
  other arithmetic  36.6 us (10%)
  matrix products  29.2 us (8%)
  starting transfers between devices  20.3 us (6%)
  between operations  16.5 us (5%)
    reduce_scatter x1, waiting for transfers between devices, body(): lax.psum_scatter(contract_first(part, back_second), ('sec', 'dev'), scatt...  167 us
    all_gather x1, waiting for transfers between devices, body(): lax.all_gather(middle_weight, ('sec', 'dev'), axis=0, tiled=True)  45 us
    dot_general x2, matrix products, contract_first(): lax.dot_general(left, right, (((0,), (0,)), ((), ())), preferred_element_...  17.4 us
    unnamed x26, local copies, waits for them, and re-layouts  12.9 us
    mul x1, other arithmetic, apply_wall(): return advanced.at[3, 0].add(-wall_gain * new_stress[1])  12.3 us
    add x1, other arithmetic, advance(): flow_state + advect_number * (below_x - flow_state)  9.62 us
    scatter x1, local copies, waits for them, and re-layouts, body(): new_stress = wall_stress.reshape(2, points).at[:, target_index].set(per_t...  7.6 us
  transfers between devices with their start and end apart: 8, of which 3 were waited for; matrix products, arithmetic and copies ran while one was open for 25% of the time, Pallas kernels for 0%

profile of v1, /device:TPU:9, one launch (start us, length us, event | category | flops | bytes accessed | tf_op | source)
XLA Modules:
  0.0 361.0 jit_solution(15559679086343298229)
XLA Ops:
  11.9 6.3 %all-to-all-start.2 = ((bf16[32,2,4]{2,1,0:T(2,128)(2,1)}), bf16[32,2,4]{2,1,0:T(2,128)(2,1)S(1)}, u32[]{:S(2)}, u32[]{:S(2)}) async-start(bf16[32,2,4]{2,1,0:T(2,128)(2,1)} %bitcast.18), calls=%async_computation.2 | async-start | bytes 32768 | tf_op jit(solution)/shard_map/all_to_all | solution.py:106
  19.1 2.0 convert_element_type.52
  22.9 3.4 copy.38
  26.2 3.4 gather_fusion
  30.8 5.8 %all-to-all-start = ((bf16[32,2,14,4]{2,1,3,0:T(2,128)(2,1)}), bf16[32,2,14,4]{2,1,3,0:T(2,128)(2,1)S(1)}, u32[]{:S(2)}, u32[]{:S(2)}) async-start(bf16[32,2,14,4]{2,1,3,0:T(2,128)(2,1)} %copy.41), calls=%async_computation | async-start | bytes 131072 | tf_op jit(solution)/shard_map/all_to_all | solution.py:105
  36.8 5.8 %all-to-all-done = bf16[32,2,14,4]{2,1,3,0:T(2,128)(2,1)S(1)} async-done(((bf16[32,2,14,4]{2,1,3,0:T(2,128)(2,1)}), bf16[32,2,14,4]{2,1,3,0:T(2,128)(2,1)S(1)}, u32[]{:S(2)}, u32[]{:S(2)}) %all-to-all-start) | async-done | bytes 7200 | tf_op jit(solution)/shard_map/all_to_all | solution.py:105
  42.9 1.7 convolution_tanh_fusion.1
  44.6 45.0 %all-gather.5.cloned.1.call-done = bf16[2048,2048]{1,0:T(8,128)(2,1)} async-done(((bf16[64,2048]{1,0:T(8,128)(2,1)}), bf16[2048,2048]{1,0:T(8,128)(2,1)}) %all-gather.5.cloned.1.call-update) | async-done | bytes 8388624 | tf_op jit(solution)/shard_map/all_gather | solution.py:118
  89.6 6.4 %convolution_tanh_fusion = f32[256,2048]{1,0:T(8,128)S(1)} fusion(bf16[2048,2048]{1,0:T(8,128)(2,1)} %all-gather.5.cloned.1.call-done, f32[256,2048]{1,0:T(8,128)} %convolution_tanh_fusion.1), kind=kOutput, calls=%fused_computation.8 | convolution fusion | flops 2148007936 | bytes 12582912 | tf_op jit(solution)/shard_map/dot_general | solution.py:116
  98.4 7.4 %convolution_bitcast_fusion = f32[1,12,2048]{2,1,0:T(8,128)} fusion(bf16[256,2048]{1,0:T(8,128)(2,1)} %fusion.8, bf16[2048,2048]{1,0:T(8,128)(2,1)} %all-gather.5.cloned.1.call-done, f32[256,2048]{1,0:T(8,128)} %convolution_tanh_fusion.1, bf16[256,14]{1,0:T(8,128)(2,1)S(1)} %bitcast.61), kind=kOutput, calls=%fused_computation.21 | convolution fusion | flops 2162163712 | bytes 11639808 | tf_op jit(solution)/shard_map/dot_general | solution.py:51
  105.9 10.0 %fusion.11 = f32[2048,2048]{1,0:T(8,128)} fusion(bf16[256,2048]{1,0:T(8,128)(2,1)} %fusion.8, f32[256,2048]{1,0:T(8,128)} %convolution_tanh_fusion.1), kind=kOutput, calls=%fused_computation.29 | convolution fusion | flops 2148007936 | bytes 19922944 | tf_op jit(solution)/shard_map/dot_general | solution.py:51
  118.7 4.6 %copy.35 = f32[2,32,512]{0,2,1:T(8,128)} copy(f32[2,32,512]{2,1,0:T(8,128)S(1)} %copy-done.5) | data formatting | bytes 262144 | tf_op args[2]
  125.4 2.8 fusion.41
  128.1 3.5 fusion.40
  132.3 3.3 maximum_convert_fusion
  136.3 6.7 %all-to-all-start.1 = ((bf16[32,2,2,4]{3,1,2,0:T(2,128)(2,1)}), bf16[32,2,2,4]{3,1,2,0:T(2,128)(2,1)S(1)}, u32[]{:S(2)}, u32[]{:S(2)}) async-start(bf16[32,2,2,4]{3,1,2,0:T(2,128)(2,1)} %copy.43), calls=%async_computation.1 | async-start | bytes 65536 | tf_op jit(solution)/shard_map/all_to_all | solution.py:128
  143.0 9.6 %fusion.4 = f32[5,8,32,512]{3,2,1,0:T(8,128)} fusion(f32[5,8,34,512]{3,2,1,0:T(8,128)} %maximum_convert_fusion, f32[5,8,32,1]{3,2,1,0:T(8,128)} %get-tuple-element.49, f32[5,8,32,511]{3,2,1,0:T(8,128)} %get-tuple-element.51, f32[5,7,32,512]{3,2,1,0:T(8,128)} %get-tuple-element.53, f32[5,1,32,512]{3,2,1,0:T(8,128)} %get-tuple-element.55, ...), kind=kLoop, calls=%fused_computation.13 | loop fusion | flops 10485760 | bytes 21495808 | tf_op jit(solution)/shard_map/add | solution.py:33
  154.5 7.6 %scatter_fusion = f32[2,16384]{0,1:T(8,128)} fusion(f32[2,16384]{0,1:T(8,128)} %bitcast.54, s32[192]{0:T(256)S(1)} %bitcast.70, f32[192,2]{1,0:T(8,128)S(1)} %copy.47), kind=kCustom, calls=%fused_computation.1 | custom fusion | bytes 5376 | tf_op jit(solution)/shard_map/scatter | solution.py:155
  162.1 5.9 %copy.50 = f32[2,32,512]{2,1,0:T(8,128)} copy(f32[2,32,512]{0,2,1:T(8,128)} %bitcast.55) | data formatting | bytes 262144
  168.1 12.3 %fusion = (f32[16384]{0:T(1024)S(1)}, f32[16384]{0:T(1024)S(1)}) fusion(f32[2,16384]{0,1:T(8,128)} %scatter_fusion), kind=kLoop, calls=%fused_computation.3 | loop fusion | flops 32768 | bytes 262144 | tf_op jit(solution)/shard_map/mul | solution.py:47
  180.4 1.5 fusion.15
  181.9 1.5 fusion.14
  183.4 3.1 reduce_sum.42
  186.5 166.9 %reduce-scatter.2.cloned.1.call-done = f32[64,2048]{1,0:T(8,128)} async-done(((f32[2048,2048]{1,0:T(8,128)}), f32[64,2048]{1,0:T(8,128)}) %reduce-scatter.2.cloned.1.call-update) | async-done | bytes 524304 | tf_op jit(solution)/shard_map/reduce_scatter | solution.py:144
  (76 shorter events, 18.1 us)
Async XLA Ops:
  7.2 35.7 %copy-start = (bf16[12,2048]{1,0:T(8,128)(2,1)S(1)}, bf16[12,2048]{1,0:T(8,128)(2,1)}, u32[]{:S(2)}) copy-start(bf16[12,2048]{1,0:T(8,128)(2,1)} %param.19) | copy-start | bytes 147460
  7.2 13.9 %copy-start.2 = (f32[5,8,32,512]{3,2,1,0:T(8,128)S(1)}, f32[5,8,32,512]{3,2,1,0:T(8,128)}, u32[]{:S(2)}) copy-start(f32[5,8,32,512]{3,2,1,0:T(8,128)} %param.13) | copy-start | bytes 7864324
  7.2 82.4 %all-gather.5.cloned.1.call-start = ((), (), s32[]{:S(2)}) async-start(), calls=%async_computation.4 | async-start | bytes 8650752 | tf_op jit(solution)/shard_map/all_gather | solution.py:118
  11.9 18.9 %all-to-all-start.2 = ((bf16[32,2,4]{2,1,0:T(2,128)(2,1)}), bf16[32,2,4]{2,1,0:T(2,128)(2,1)S(1)}, u32[]{:S(2)}, u32[]{:S(2)}) async-start(bf16[32,2,4]{2,1,0:T(2,128)(2,1)} %bitcast.18), calls=%async_computation.2 | async-start | bytes 32768 | tf_op jit(solution)/shard_map/all_to_all | solution.py:106
  21.1 1.1 copy-start.3
  22.8 6.9 %copy-start.7 = (s32[48,4]{0,1:T(4,128)S(1)}, s32[48,4]{0,1:T(4,128)}, u32[]{:S(2)}) copy-start(s32[48,4]{0,1:T(4,128)} %param.18) | copy-start | bytes 2308
  22.8 6.9 %copy-start.8 = (s32[1,48]{1,0:T(1,128)S(1)}, s32[1,48]{1,0:T(1,128)}, u32[]{:S(2)}) copy-start(s32[1,48]{1,0:T(1,128)} %param.16) | copy-start | bytes 580
  30.8 11.8 %all-to-all-start = ((bf16[32,2,14,4]{2,1,3,0:T(2,128)(2,1)}), bf16[32,2,14,4]{2,1,3,0:T(2,128)(2,1)S(1)}, u32[]{:S(2)}, u32[]{:S(2)}) async-start(bf16[32,2,14,4]{2,1,3,0:T(2,128)(2,1)} %copy.41), calls=%async_computation | async-start | bytes 131072 | tf_op jit(solution)/shard_map/all_to_all | solution.py:105
  36.7 146.7 %all-gather.7.cloned.1.call-start = ((), (), s32[]{:S(2)}) async-start(), calls=%async_computation.6 | async-start | bytes 4325376 | tf_op jit(solution)/shard_map/all_gather | solution.py:148
  44.6 51.3 %copy-start.6 = (bf16[2,2048]{1,0:T(2,128)(2,1)S(1)}, bf16[2,2048]{1,0:T(2,128)(2,1)}, u32[]{:S(2)}) copy-start(bf16[2,2048]{1,0:T(2,128)(2,1)} %param.21) | copy-start | bytes 24580
  105.8 247.5 %reduce-scatter.2.cloned.1.call-start = ((), (), s32[]{:S(2)}) async-start(), calls=%async_computation.5 | async-start | bytes 17301504 | tf_op jit(solution)/shard_map/reduce_scatter | solution.py:144
  115.9 2.8 copy-start.5
  117.1 15.1 %collective-permute-start = (bf16[5,8,1,512]{3,2,1,0:T(2,128)(2,1)S(1)}, bf16[5,8,1,512]{3,2,1,0:T(2,128)(2,1)}, u32[]{:S(2)}, u32[]{:S(2)}) collective-permute-start(bf16[5,8,1,512]{3,2,1,0:T(2,128)(2,1)S(1)} %get-tuple-element.56), channel_id=1, source_target_pairs={{0,1},{1,2},{2,3},{3,4},{4,5},{5,6},{6,7},{7,8},{8,9},{9,10},{10,1... | collective-permute-start | bytes 122888 | tf_op jit(solution)/shard_map/ppermute | solution.py:19
  118.5 13.8 %collective-permute-start.1 = (bf16[5,8,1,512]{3,2,1,0:T(2,128)(2,1)S(1)}, bf16[5,8,1,512]{3,2,1,0:T(2,128)(2,1)}, u32[]{:S(2)}, u32[]{:S(2)}) collective-permute-start(bf16[5,8,1,512]{3,2,1,0:T(2,128)(2,1)S(1)} %get-tuple-element.57), channel_id=1, source_target_pairs={{1,0},{2,1},{3,2},{4,3},{5,4},{6,5},{7,6},{8,7},{9,8},{10,9},{11,1... | collective-permute-start | bytes 122888 | tf_op jit(solution)/shard_map/ppermute | solution.py:22
  128.1 4.1 %copy-start.4 = (bf16[5,8,32,512]{3,2,1,0:T(8,128)(2,1)S(1)}, bf16[5,8,32,512]{3,2,1,0:T(8,128)(2,1)}, u32[]{:S(2)}) copy-start(bf16[5,8,32,512]{3,2,1,0:T(8,128)(2,1)} %copy-done.3) | copy-start | bytes 3932164
  136.3 17.6 %all-to-all-start.1 = ((bf16[32,2,2,4]{3,1,2,0:T(2,128)(2,1)}), bf16[32,2,2,4]{3,1,2,0:T(2,128)(2,1)S(1)}, u32[]{:S(2)}, u32[]{:S(2)}) async-start(bf16[32,2,2,4]{3,1,2,0:T(2,128)(2,1)} %copy.43), calls=%async_computation.1 | async-start | bytes 65536 | tf_op jit(solution)/shard_map/all_to_all | solution.py:128
  168.1 185.3 %copy-start.1 = (bf16[12,2048]{1,0:T(8,128)(2,1)S(1)}, bf16[12,2048]{1,0:T(8,128)(2,1)}, u32[]{:S(2)}) copy-start(bf16[12,2048]{1,0:T(8,128)(2,1)} %param.19) | copy-start | bytes 147460
Sparse Core Ops, SparseCore 0:
  10.8 78.6 all-gather.4
  106.0 60.1 all-gather.6
  169.0 184.2 reduce-scatter.1
